TPU v7x, 128 devices: a whole 4x4x4 slice. The times are simulated.
128 devices in a mesh: row: 16 (over y_hi, x, core), col: 8 (over y_lo, z).
Axes of the slice: x: 4, y: 4 (y_hi: 2, y_lo: 2; y = y_hi * 2 + y_lo), z: 4, core: 2. Of those that a mesh axis runs over, the one named last changes fastest.
Arguments:
- gradient: float32 [2048, 14336], P('row', 'col'), may hold values from -6 to 6
- precond: bfloat16 [14336, 14336], P('row', 'col'), as said below
Outputs:
- direction: float32 [2048, 14336], P('row', 'col')
Inputs may be any that keep to these rules, and one draw needn't show every extreme that they name: precond is symmetric, and its diagonal is positive and larger than any off-diagonal entry in the same row (the matrix is not diagonally dominant: the off-diagonal entries together outweigh the diagonal).
All inputs are finite; a program needn't handle non-finite values.
Results may differ from a plain program's by a relative error of at most 0.0039.
Values may be sent and summed in bfloat16 or wider, within the bound.
A program may use at most 64 MiB of HBM per device.

v0:
```python
import jax
import jax.numpy as jnp
from jax import lax
from jax.sharding import PartitionSpec as P


def local(gradient, precond):
    grad_low = gradient.astype(jnp.bfloat16)
    partial_value = lax.dot_general(
        lax.all_gather(grad_low, "row", axis=0, tiled=True),
        precond,
        (((1,), (1,)), ((), ())),
        preferred_element_type=jnp.float32,
    )
    first = lax.psum(partial_value, "col").astype(jnp.bfloat16)
    product = jnp.dot(first, precond, preferred_element_type=jnp.float32)
    direction = lax.psum_scatter(product, "row", scatter_dimension=0, tiled=True)
    return direction


def solution(mesh):
    placed = (P("row", "col"), P("row", "col"))
    return jax.shard_map(
        local, mesh=mesh, in_specs=placed, out_specs=P("row", "col"), check_vma=False
    )
```

profile of v0, /device:TPU:0, one launch (start us, length us, event | category | flops | bytes accessed | tf_op | source)
XLA Modules:
  0.0 392.0 jit_solution(10136501896560998755)
XLA Ops:
  6.5 0.0 copy-start
  6.5 0.0 all-gather.2.cloned.1.call-start
  6.5 2.1 convert_element_type.6
  8.7 0.0 all-gather.2.cloned.1.call-update
  8.7 0.0 reduce-scatter.2.cloned.1.call-start
  8.8 71.8 %all-gather.2.cloned.1.call-done = bf16[2048,1792]{1,0:T(8,128)(2,1)} async-done(((bf16[128,1792]{1,0:T(8,128)(2,1)}), bf16[2048,1792]{1,0:T(8,128)(2,1)}) %all-gather.2.cloned.1.call-update) | async-done | bytes 7340048 | tf_op jit(solution)/shard_map/all_gather | solution.py:10
  80.6 0.0 copy-done
  80.6 11.8 %fusion.2 = f32[2048,896]{1,0:T(8,128)} fusion(bf16[2048,1792]{1,0:T(8,128)(2,1)} %all-gather.2.cloned.1.call-done, bf16[896,1792]{1,0:T(8,128)(2,1)S(1)} %copy-done), kind=kOutput, calls=%fused_computation.2 | convolution fusion | flops 6576668672 | bytes 17891328 | tf_op jit(solution)/shard_map/dot_general | solution.py:9
  92.4 151.4 %all-reduce.1 = bf16[2048,896]{1,0:T(8,128)(2,1)} all-reduce(f32[2048,896]{1,0:T(8,128)} %fusion.2), channel_id=1, replica_groups=mesh['row'=16,'col'=8] {'col'}, use_global_device_ids=true, to_apply=%region_0.0 | all-reduce | flops 1835008 | bytes 11010048 | tf_op jit(solution)/shard_map/psum | solution.py:15
  243.9 12.4 %fusion.3 = f32[2048,1792]{1,0:T(8,128)} fusion(bf16[2048,896]{1,0:T(8,128)(2,1)} %all-reduce.1, bf16[896,1792]{1,0:T(8,128)(2,1)S(1)} %copy-done), kind=kOutput, calls=%fused_computation.3 | convolution fusion | flops 6576668672 | bytes 21561344 | tf_op jit(solution)/shard_map/dot_general | solution.py:16
  256.3 0.0 reduce-scatter.2.cloned.1.call-update
  256.3 128.9 %reduce-scatter.2.cloned.1.call-done = f32[128,1792]{1,0:T(8,128)} async-done(((f32[2048,1792]{1,0:T(8,128)}), f32[128,1792]{1,0:T(8,128)}) %reduce-scatter.2.cloned.1.call-update) | async-done | bytes 917520 | tf_op jit(solution)/shard_map/reduce_scatter | solution.py:17
Async XLA Ops:
  6.5 74.1 %copy-start = (bf16[896,1792]{1,0:T(8,128)(2,1)S(1)}, bf16[896,1792]{1,0:T(8,128)(2,1)}, u32[]{:S(2)}) copy-start(bf16[896,1792]{1,0:T(8,128)(2,1)} %param.3) | copy-start | bytes 9633796
  6.5 74.1 %all-gather.2.cloned.1.call-start = ((), (), s32[]{:S(2)}) async-start(), calls=%async_computation.1 | async-start | bytes 7798784 | tf_op jit(solution)/shard_map/all_gather | solution.py:10
  8.7 376.5 %reduce-scatter.2.cloned.1.call-start = ((), (), s32[]{:S(2)}) async-start(), calls=%async_computation.2 | async-start | bytes 15597568 | tf_op jit(solution)/shard_map/reduce_scatter | solution.py:17
Sparse Core Ops, SparseCore 0:
  9.8 70.7 all-gather.1
  256.4 128.6 reduce-scatter.1
where the time goes:
time: 392 us
  waiting for transfers between devices  201 us (51%)
  blocking collectives  151 us (39%)
  matrix products  24.3 us (6%)
  between operations  13.4 us (3%)
    psum x1, blocking collectives, local(): first = lax.psum(partial_value, 'col').astype(jnp.bfloat16)  151 us
    reduce_scatter x1, waiting for transfers between devices, local(): lax.psum_scatter(product, 'row', scatter_dimension=0, tiled=True)  129 us
    all_gather x1, waiting for transfers between devices, local(): lax.all_gather(grad_low, 'row', axis=0, tiled=True)  71.8 us
    dot_general x1, matrix products, local(): product = jnp.dot(first, precond, preferred_element_type=jnp.float32)  12.4 us
    dot_general x1, matrix products, local(): lax.dot_general(lax.all_gather(grad_low, 'row', axis=0, tiled=True), prec...  11.8 us
  transfers between devices with their start and end apart: 2, of which 2 were waited for; matrix products, arithmetic and copies ran while one was open for 0% of the time, Pallas kernels for 0%

commit v1 on v0

v1 whole, which is shorter than its diff:
```python
import functools

import jax
import jax.numpy as jnp
from jax import lax
from jax.experimental import pallas as pl
from jax.experimental.pallas import tpu as pltpu
from jax.sharding import PartitionSpec as P

MESH = pl.DeviceIdType.MESH
BF16, F32 = jnp.bfloat16, jnp.float32

W = 64
TILE = 256
RING = 4

GATHER_X, SEND_G, SCATTER_Z, PAIR, GATHER_Z, SCATTER_X, SEND_OUT, KINDS = 0, 4, 5, 11, 12, 16, 22, 23

ORDER = (
    ("enter", -2), ("relay", -1), ("first", 0), ("to_pair", 1), ("second", 3), ("hop1", 0), ("round_first", 1),
    ("hop2", 3), ("relay2", 2), ("end", 4),
)


def kernel(rows, g_hbm, q_hbm, out, g_wide, factor, gath, part, own, hop_s, plus_s, minus_s, hop_r, plus_r,
           minus_r, pair_s, pair_r, mid, part2, own2, hop2_s, plus2_s, minus2_s, hop2_r, plus2_r, minus2_r,
           out_s, out_r, local_sem, core_send, core_recv, ss, rs):
    half_chunks = rows // W
    chunks = 2 * half_chunks
    early = half_chunks // 2
    r, c = lax.axis_index("row"), lax.axis_index("col")
    core = r % 2
    x = (r // 2) % RING
    yh = r // (2 * RING)
    z = c % RING
    yl = c // RING

    def at(yh, x, core, yl, z):
        return ((yh * RING + x) * 2 + core, yl * RING + z)

    xr, xl, xo = (x + 1) % RING, (x + 3) % RING, (x + 2) % RING
    zr, zl, zo = (z + 1) % RING, (z + 3) % RING, (z + 2) % RING
    x_plus, x_minus = at(yh, xr, core, yl, z), at(yh, xl, core, yl, z)
    z_plus, z_minus = at(yh, x, core, yl, zr), at(yh, x, core, yl, zl)
    far = at(1 - yh, x, core, yl, z)
    pair = at(yh, x, core, 1 - yl, z)
    twin = at(yh, x, 1 - core, yl, z)

    depth = q_hbm.shape[0]
    mine = pl.ds(pl.multiple_of(core * depth, depth), depth)
    theirs = pl.ds(pl.multiple_of((1 - core) * depth, depth), depth)
    top, low = pl.ds(0, W // 2), pl.ds(W // 2, W // 2)

    load_g = pltpu.make_async_copy(g_hbm, g_wide, local_sem.at[0])
    load_q = pltpu.make_async_copy(q_hbm, factor.at[mine], local_sem.at[1])
    load_g.start()
    load_q.start()

    barrier = pltpu.get_barrier_semaphore()
    for device in (x_plus, x_minus, z_plus, z_minus, far, pair, twin):
        pl.semaphore_signal(barrier, inc=1, device_id=device, device_id_type=MESH)
    pl.semaphore_wait(barrier, 7)

    share = pltpu.make_async_remote_copy(
        src_ref=q_hbm, dst_ref=factor.at[mine], send_sem=core_send, recv_sem=core_recv,
        device_id=twin, device_id_type=MESH)
    share.start()

    def copy(kind, i, src, dst, device):
        return pltpu.make_async_remote_copy(
            src_ref=src, dst_ref=dst, send_sem=ss.at[kind, i], recv_sem=rs.at[kind, i],
            device_id=device, device_id_type=MESH)

    def gather_send(kind, i, buf, me, plus, minus):
        copy(kind, i, buf.at[i, me], buf.at[i, me], plus).start()
        copy(kind + 1, i, buf.at[i, me], buf.at[i, me], minus).start()

    def gather_relay(kind, i, buf, left, right, plus, minus):
        copy(kind, i, buf.at[i, left], buf.at[i, left], plus).wait_recv()
        copy(kind + 2, i, buf.at[i, left, top], buf.at[i, left, top], plus).start()
        copy(kind + 1, i, buf.at[i, right], buf.at[i, right], minus).wait_recv()
        copy(kind + 3, i, buf.at[i, right, low], buf.at[i, right, low], minus).start()

    def gather_wait(kind, i, buf, across, plus, minus):
        copy(kind + 2, i, buf.at[i, across, top], buf.at[i, across, top], plus).wait_recv()
        copy(kind + 3, i, buf.at[i, across, low], buf.at[i, across, low], minus).wait_recv()

    def scatter_send(kind, i, p, mine_f, hs, ps, ms, hr, pr, mr, me, left, right, across, plus, minus):
        hs[i] = p[across].astype(BF16)
        copy(kind, i, hs.at[i, top], hr.at[i, top], plus).start()
        copy(kind + 1, i, hs.at[i, low], hr.at[i, low], minus).start()
        ps[i, W // 2:] = p[right, W // 2:].astype(BF16)
        copy(kind + 2, i, ps.at[i, low], pr.at[i, low], plus).start()
        ms[i, : W // 2] = p[left, : W // 2].astype(BF16)
        copy(kind + 3, i, ms.at[i, top], mr.at[i, top], minus).start()
        mine_f[i] = p[me]

    def scatter_hop(kind, i, p, hs, ps, ms, hr, pr, mr, left, right, plus, minus):
        copy(kind, i, hs.at[i, top], hr.at[i, top], plus).wait_recv()
        ps[i, : W // 2] = (p[right, : W // 2] + hr[i, : W // 2].astype(F32)).astype(BF16)
        copy(kind + 4, i, ps.at[i, top], pr.at[i, top], plus).start()
        copy(kind + 1, i, hs.at[i, low], hr.at[i, low], minus).wait_recv()
        ms[i, W // 2:] = (p[left, W // 2:] + hr[i, W // 2:].astype(F32)).astype(BF16)
        copy(kind + 5, i, ms.at[i, low], mr.at[i, low], minus).start()

    def scatter_wait(kind, i, mine_f, ps, ms, pr, mr, plus, minus):
        copy(kind + 2, i, ps.at[i, low], pr.at[i, low], plus).wait_recv()
        copy(kind + 3, i, ms.at[i, top], mr.at[i, top], minus).wait_recv()
        copy(kind + 4, i, ps.at[i, top], pr.at[i, top], plus).wait_recv()
        copy(kind + 5, i, ms.at[i, low], mr.at[i, low], minus).wait_recv()
        return mine_f[i] + pr[i].astype(F32) + mr[i].astype(F32)

    load_g.wait()
    for q in range(half_chunks):
        i = q if q < early else half_chunks + q
        gath[i, x] = g_wide[q * W:(q + 1) * W].astype(BF16)
        gather_send(GATHER_X, i, gath, x, x_plus, x_minus)
        copy(SEND_G, early + q, gath.at[i, x], gath.at[early + q, x], far).start()
    load_q.wait()

    width = factor.shape[1]

    def stage(step, lag, fn):
        i = step - lag

        @pl.when((i >= 0) & (i < chunks))
        def _():
            fn(i)

    def is_far(i):
        return (i >= early) & (i < early + half_chunks)

    def enter(i):
        @pl.when(is_far(i))
        def _():
            copy(SEND_G, i, gath.at[i, x], gath.at[i, x], far).wait_recv()
            gather_send(GATHER_X, i, gath, x, x_plus, x_minus)

    def relay(i):
        gather_relay(GATHER_X, i, gath, xl, xr, x_plus, x_minus)

    def first(i):
        gather_wait(GATHER_X, i, gath, xo, x_plus, x_minus)

        @pl.when(i == 0)
        def _():
            pltpu.make_async_remote_copy(
                src_ref=q_hbm, dst_ref=factor.at[theirs], send_sem=core_send, recv_sem=core_recv,
                device_id=twin, device_id_type=MESH).wait_recv()

        lhs = gath[i].reshape(RING * W, width)
        for t in range(0, width, TILE):
            value = lax.dot_general(lhs, factor[t:t + TILE, :], (((1,), (1,)), ((), ())), preferred_element_type=F32)
            part[:, :, t:t + TILE] = value.reshape(RING, W, TILE)
        scatter_send(SCATTER_Z, i, part, own, hop_s, plus_s, minus_s, hop_r, plus_r, minus_r,
                     z, zl, zr, zo, z_plus, z_minus)

    def hop1(i):
        scatter_hop(SCATTER_Z, i, part, hop_s, plus_s, minus_s, hop_r, plus_r, minus_r, zl, zr, z_plus, z_minus)

    def to_pair(i):
        value = scatter_wait(SCATTER_Z, i, own, plus_s, minus_s, plus_r, minus_r, z_plus, z_minus)
        own[i] = value
        pair_s[i] = value.astype(BF16)
        copy(PAIR, i, pair_s.at[i], pair_r.at[i], pair).start()

    def round_first(i):
        copy(PAIR, i, pair_s.at[i], pair_r.at[i], pair).wait_recv()
        mid[i, z] = (own[i] + pair_r[i].astype(F32)).astype(BF16)
        gather_send(GATHER_Z, i, mid, z, z_plus, z_minus)

    def relay2(i):
        gather_relay(GATHER_Z, i, mid, zl, zr, z_plus, z_minus)

    def second(i):
        gather_wait(GATHER_Z, i, mid, zo, z_plus, z_minus)
        lhs = mid[i].reshape(RING * W, width)
        for t in range(0, width, TILE):
            value = jnp.dot(lhs, factor[:, t:t + TILE], preferred_element_type=F32)
            part2[:, :, t:t + TILE] = value.reshape(RING, W, TILE)
        scatter_send(SCATTER_X, i, part2, own2, hop2_s, plus2_s, minus2_s, hop2_r, plus2_r, minus2_r,
                     x, xl, xr, xo, x_plus, x_minus)

    def hop2(i):
        scatter_hop(SCATTER_X, i, part2, hop2_s, plus2_s, minus2_s, hop2_r, plus2_r, minus2_r,
                    xl, xr, x_plus, x_minus)

    def end(i):
        value = scatter_wait(SCATTER_X, i, own2, plus2_s, minus2_s, plus2_r, minus2_r, x_plus, x_minus)

        @pl.when(is_far(i))
        def _():
            out_s[i - early] = value.astype(BF16)
            copy(SEND_OUT, i - early, out_s.at[i - early], out_r.at[i - early], far).start()

        @pl.when(jnp.logical_not(is_far(i)))
        def _():
            q = jnp.where(i < early, i, i - half_chunks)
            out[pl.ds(pl.multiple_of(q * W, W), W), :] = value

    stages = {
        "enter": enter, "relay": relay, "first": first, "hop1": hop1, "to_pair": to_pair,
        "round_first": round_first, "relay2": relay2, "second": second, "hop2": hop2, "end": end,
    }
    lags = [lag for _, lag in ORDER]

    def loop(step, carry):
        for name, lag in ORDER:
            stage(step, lag, stages[name])
        return carry

    lax.fori_loop(min(lags), chunks + max(lags), loop, 0)

    for q in range(half_chunks):
        copy(SEND_OUT, q, out_s.at[q], out_r.at[q], far).wait_recv()
        out[q * W:(q + 1) * W] += out_r[q].astype(F32)

    share.wait_send()

    def drain(i, carry):
        for kind, buf in ((GATHER_X, gath), (GATHER_Z, mid)):
            for k, piece in enumerate((buf.at[i, 0], buf.at[i, 0], buf.at[i, 0, top], buf.at[i, 0, low])):
                copy(kind + k, i, piece, piece, x_plus).wait_send()
        for kind in (SCATTER_Z, SCATTER_X):
            for k in range(6):
                copy(kind + k, i, hop_s.at[i, top], hop_s.at[i, top], x_plus).wait_send()
        copy(PAIR, i, pair_s.at[i], pair_s.at[i], pair).wait_send()

        @pl.when(i < half_chunks)
        def _():
            copy(SEND_G, early + i, pair_s.at[i], pair_s.at[i], far).wait_send()
            copy(SEND_OUT, i, out_s.at[i], out_s.at[i], far).wait_send()

        return carry

    lax.fori_loop(0, chunks, drain, 0)


def local(gradient, precond):
    rows, width = gradient.shape
    chunks = 2 * rows // W
    block = pltpu.VMEM((chunks, W, width), BF16)
    wide = pltpu.VMEM((chunks, W, width), F32)
    ring = pltpu.VMEM((chunks, RING, W, width), BF16)
    part = pltpu.VMEM((RING, W, width), F32)
    out_block = pltpu.VMEM((chunks // 2, W, width), BF16)
    return pl.pallas_call(
        functools.partial(kernel, rows),
        out_shape=jax.ShapeDtypeStruct((rows, width), F32),
        in_specs=[pl.BlockSpec(memory_space=pl.ANY)] * 2,
        out_specs=pl.BlockSpec(memory_space=pltpu.VMEM),
        scratch_shapes=[
            pltpu.VMEM((rows, width), F32),
            pltpu.VMEM((2 * precond.shape[0], width), BF16),
            ring, part, wide, block, block, block, block, block, block, block, block,
            ring, part, wide, block, block, block, block, block, block,
            out_block, out_block,
            pltpu.SemaphoreType.DMA((2,)),
            pltpu.SemaphoreType.DMA,
            pltpu.SemaphoreType.DMA,
            pltpu.SemaphoreType.DMA((KINDS, chunks)),
            pltpu.SemaphoreType.DMA((KINDS, chunks)),
        ],
        compiler_params=pltpu.CompilerParams(
            collective_id=0, has_side_effects=True, vmem_limit_bytes=60 * 1024 * 1024
        ),
    )(gradient, precond)


def solution(mesh):
    placed = (P("row", "col"), P("row", "col"))
    return jax.shard_map(
        local, mesh=mesh, in_specs=placed, out_specs=P("row", "col"), check_vma=False
    )
```

time: 392 us -> 118 us (0.30)
  waiting for transfers between devices: 201 us -> 0 us
  blocking collectives: 151 us -> 0 us
  Pallas kernels: 0 us -> 116 us
  matrix products: 24.3 us -> 0 us
  between operations: 13.4 us -> 0.01 us
    psum x1 -> x0, blocking collectives: 151 us -> none  [local(): first = lax.psum(partial_value, 'col').astype(jnp.bfloat16)]
    reduce_scatter x1 -> x0, waiting for transfers between devices: 129 us -> none  [local(): lax.psum_scatter(product, 'row', scatter_dimension=0, tiled=True)]
    pallas_call x0 -> x1, Pallas kernels: none -> 116 us  [local(): pl.pallas_call(functools.partial(kernel, rows), out_shape=jax.ShapeDtypeS...]
    all_gather x1 -> x0, waiting for transfers between devices: 71.8 us -> none  [local(): lax.all_gather(grad_low, 'row', axis=0, tiled=True)]
    dot_general x2 -> x0, matrix products: 24.3 us -> none  [the longest x1 12.4 us: local(): product = jnp.dot(first, precond, preferred_element_type=jnp.float32)]
  transfers between devices with their start and end apart: 2 -> 0, of which waited for: 2 -> 0; matrix products, arithmetic and copies ran while one was open for 0% -> 0% of each run, Pallas kernels for 0% -> 0%
where the time goes in v1:
time: 118 us
  Pallas kernels  116 us (98%)
  local copies, waits for them, and re-layouts  2.16 us (2%)
    pallas_call x1, Pallas kernels, local(): pl.pallas_call(functools.partial(kernel, rows), out_shape=jax.ShapeDtypeS...  116 us

profile of v1, /device:TPU:0, one launch (start us, length us, event | category | flops | bytes accessed | tf_op | source)
XLA Modules:
  0.0 117.8 jit_solution(11687939088263055944)
XLA Ops:
  0.0 115.6 %shard_map.28 = f32[128,1792]{1,0:T(8,128)} custom-call(f32[128,1792]{1,0:T(8,128)} %g_hbm.1, bf16[896,1792]{1,0:T(8,128)(2,1)} %q_hbm.1), custom_call_target="tpu_custom_call" | custom-call | tf_op jit(solution)/shard_map/pallas_call | solution.py:247
  115.6 2.2 %copy.4 = f32[128,1792]{1,0:T(8,128)} copy(f32[128,1792]{1,0:T(8,128)} %shard_map.28) | data formatting | bytes 1835008

commit v2 on v1

--- a/solution.py
+++ b/solution.py
@@ -10,20 +10,41 @@
 MESH = pl.DeviceIdType.MESH
 BF16, F32 = jnp.bfloat16, jnp.float32
 
-W = 64
+W = 32
 TILE = 256
+SPAN = 30
 RING = 4
 
 GATHER_X, SEND_G, SCATTER_Z, PAIR, GATHER_Z, SCATTER_X, SEND_OUT, KINDS = 0, 4, 5, 11, 12, 16, 22, 23
 
 ORDER = (
-    ("enter", -2), ("relay", -1), ("first", 0), ("to_pair", 1), ("second", 3), ("hop1", 0), ("round_first", 1),
-    ("hop2", 3), ("relay2", 2), ("end", 4),
+    "enter",
+    "first",
+    "round_first",
+    "relay",
+    "to_pair",
+    "hop2",
+    "second",
+    "hop1",
+    "relay2",
+    "end",
 )
-
-
-def kernel(rows, g_hbm, q_hbm, out, g_wide, factor, gath, part, own, hop_s, plus_s, minus_s, hop_r, plus_r,
-           minus_r, pair_s, pair_r, mid, part2, own2, hop2_s, plus2_s, minus2_s, hop2_r, plus2_r, minus2_r,
+STEPS = {
+    "enter": (0, 1, 2, 3, 4, 5, 6, 7),
+    "first": (3, 4, 7, 8, 12, 14, 15, 17),
+    "round_first": (10, 11, 12, 14, 20, 23, 27, 28),
+    "relay": (1, 2, 3, 4, 7, 8, 9, 10),
+    "to_pair": (8, 9, 10, 13, 19, 21, 25, 26),
+    "hop2": (18, 21, 22, 26, 30, 31, 33, 34),
+    "second": (15, 16, 19, 24, 27, 29, 31, 32),
+    "hop1": (4, 7, 8, 9, 14, 16, 20, 22),
+    "relay2": (12, 13, 14, 17, 24, 26, 29, 30),
+    "end": (19, 22, 23, 28, 31, 32, 34, 35),
+}
+
+
+def kernel(rows, g_hbm, q_hbm, out, g_wide, factor, gath, part, hop_s, plus_s, minus_s, hop_r, plus_r,
+           minus_r, pair_s, pair_r, mid, part2, hop2_s, plus2_s, minus2_s, hop2_r, plus2_r, minus2_r,
            out_s, out_r, local_sem, core_send, core_recv, ss, rs):
     half_chunks = rows // W
     chunks = 2 * half_chunks
@@ -85,48 +106,41 @@
         copy(kind + 2, i, buf.at[i, across, top], buf.at[i, across, top], plus).wait_recv()
         copy(kind + 3, i, buf.at[i, across, low], buf.at[i, across, low], minus).wait_recv()
 
-    def scatter_send(kind, i, p, mine_f, hs, ps, ms, hr, pr, mr, me, left, right, across, plus, minus):
-        hs[i] = p[across].astype(BF16)
+    def scatter_send(kind, i, p, hs, ps, ms, hr, pr, mr, left, right, across, plus, minus):
+        hs[i] = p[i, across].astype(BF16)
         copy(kind, i, hs.at[i, top], hr.at[i, top], plus).start()
         copy(kind + 1, i, hs.at[i, low], hr.at[i, low], minus).start()
-        ps[i, W // 2:] = p[right, W // 2:].astype(BF16)
+        ps[i, W // 2:] = p[i, right, W // 2:].astype(BF16)
         copy(kind + 2, i, ps.at[i, low], pr.at[i, low], plus).start()
-        ms[i, : W // 2] = p[left, : W // 2].astype(BF16)
+        ms[i, : W // 2] = p[i, left, : W // 2].astype(BF16)
         copy(kind + 3, i, ms.at[i, top], mr.at[i, top], minus).start()
-        mine_f[i] = p[me]
 
     def scatter_hop(kind, i, p, hs, ps, ms, hr, pr, mr, left, right, plus, minus):
         copy(kind, i, hs.at[i, top], hr.at[i, top], plus).wait_recv()
-        ps[i, : W // 2] = (p[right, : W // 2] + hr[i, : W // 2].astype(F32)).astype(BF16)
+        ps[i, : W // 2] = (p[i, right, : W // 2] + hr[i, : W // 2].astype(F32)).astype(BF16)
         copy(kind + 4, i, ps.at[i, top], pr.at[i, top], plus).start()
         copy(kind + 1, i, hs.at[i, low], hr.at[i, low], minus).wait_recv()
-        ms[i, W // 2:] = (p[left, W // 2:] + hr[i, W // 2:].astype(F32)).astype(BF16)
+        ms[i, W // 2:] = (p[i, left, W // 2:] + hr[i, W // 2:].astype(F32)).astype(BF16)
         copy(kind + 5, i, ms.at[i, low], mr.at[i, low], minus).start()
 
-    def scatter_wait(kind, i, mine_f, ps, ms, pr, mr, plus, minus):
+    def scatter_wait(kind, i, p, me, ps, ms, pr, mr, plus, minus):
         copy(kind + 2, i, ps.at[i, low], pr.at[i, low], plus).wait_recv()
         copy(kind + 3, i, ms.at[i, top], mr.at[i, top], minus).wait_recv()
         copy(kind + 4, i, ps.at[i, top], pr.at[i, top], plus).wait_recv()
         copy(kind + 5, i, ms.at[i, low], mr.at[i, low], minus).wait_recv()
-        return mine_f[i] + pr[i].astype(F32) + mr[i].astype(F32)
+        return p[i, me] + pr[i].astype(F32) + mr[i].astype(F32)
 
     load_g.wait()
     for q in range(half_chunks):
         i = q if q < early else half_chunks + q
         gath[i, x] = g_wide[q * W:(q + 1) * W].astype(BF16)
-        gather_send(GATHER_X, i, gath, x, x_plus, x_minus)
+        if i == 0:
+            gather_send(GATHER_X, i, gath, x, x_plus, x_minus)
         copy(SEND_G, early + q, gath.at[i, x], gath.at[early + q, x], far).start()
     load_q.wait()
 
     width = factor.shape[1]
 
-    def stage(step, lag, fn):
-        i = step - lag
-
-        @pl.when((i >= 0) & (i < chunks))
-        def _():
-            fn(i)
-
     def is_far(i):
         return (i >= early) & (i < early + half_chunks)
 
@@ -134,6 +148,9 @@
         @pl.when(is_far(i))
         def _():
             copy(SEND_G, i, gath.at[i, x], gath.at[i, x], far).wait_recv()
+
+        @pl.when(i > 0)
+        def _():
             gather_send(GATHER_X, i, gath, x, x_plus, x_minus)
 
     def relay(i):
@@ -151,22 +168,22 @@
         lhs = gath[i].reshape(RING * W, width)
         for t in range(0, width, TILE):
             value = lax.dot_general(lhs, factor[t:t + TILE, :], (((1,), (1,)), ((), ())), preferred_element_type=F32)
-            part[:, :, t:t + TILE] = value.reshape(RING, W, TILE)
-        scatter_send(SCATTER_Z, i, part, own, hop_s, plus_s, minus_s, hop_r, plus_r, minus_r,
-                     z, zl, zr, zo, z_plus, z_minus)
+            part[i, :, :, t:t + TILE] = value.reshape(RING, W, TILE)
+        scatter_send(SCATTER_Z, i, part, hop_s, plus_s, minus_s, hop_r, plus_r, minus_r,
+                     zl, zr, zo, z_plus, z_minus)
 
     def hop1(i):
         scatter_hop(SCATTER_Z, i, part, hop_s, plus_s, minus_s, hop_r, plus_r, minus_r, zl, zr, z_plus, z_minus)
 
     def to_pair(i):
-        value = scatter_wait(SCATTER_Z, i, own, plus_s, minus_s, plus_r, minus_r, z_plus, z_minus)
-        own[i] = value
+        value = scatter_wait(SCATTER_Z, i, part, z, plus_s, minus_s, plus_r, minus_r, z_plus, z_minus)
+        part[i, z] = value
         pair_s[i] = value.astype(BF16)
         copy(PAIR, i, pair_s.at[i], pair_r.at[i], pair).start()
 
     def round_first(i):
         copy(PAIR, i, pair_s.at[i], pair_r.at[i], pair).wait_recv()
-        mid[i, z] = (own[i] + pair_r[i].astype(F32)).astype(BF16)
+        mid[i, z] = (part[i, z] + pair_r[i].astype(F32)).astype(BF16)
         gather_send(GATHER_Z, i, mid, z, z_plus, z_minus)
 
     def relay2(i):
@@ -177,16 +194,16 @@
         lhs = mid[i].reshape(RING * W, width)
         for t in range(0, width, TILE):
             value = jnp.dot(lhs, factor[:, t:t + TILE], preferred_element_type=F32)
-            part2[:, :, t:t + TILE] = value.reshape(RING, W, TILE)
-        scatter_send(SCATTER_X, i, part2, own2, hop2_s, plus2_s, minus2_s, hop2_r, plus2_r, minus2_r,
-                     x, xl, xr, xo, x_plus, x_minus)
+            part2[i, :, :, t:t + TILE] = value.reshape(RING, W, TILE)
+        scatter_send(SCATTER_X, i, part2, hop2_s, plus2_s, minus2_s, hop2_r, plus2_r, minus2_r,
+                     xl, xr, xo, x_plus, x_minus)
 
     def hop2(i):
         scatter_hop(SCATTER_X, i, part2, hop2_s, plus2_s, minus2_s, hop2_r, plus2_r, minus2_r,
                     xl, xr, x_plus, x_minus)
 
     def end(i):
-        value = scatter_wait(SCATTER_X, i, own2, plus2_s, minus2_s, plus2_r, minus2_r, x_plus, x_minus)
+        value = scatter_wait(SCATTER_X, i, part2, x, plus2_s, minus2_s, plus2_r, minus2_r, x_plus, x_minus)
 
         @pl.when(is_far(i))
         def _():
@@ -202,14 +219,30 @@
         "enter": enter, "relay": relay, "first": first, "hop1": hop1, "to_pair": to_pair,
         "round_first": round_first, "relay2": relay2, "second": second, "hop2": hop2, "end": end,
     }
-    lags = [lag for _, lag in ORDER]
+    total = 1 + max(max(at_steps) for at_steps in STEPS.values())
+    words = [
+        [sum(1 << (t - w) for t in STEPS[name] if w <= t < w + SPAN) for w in range(0, total, SPAN)]
+        for name in ORDER
+    ]
 
     def loop(step, carry):
-        for name, lag in ORDER:
-            stage(step, lag, stages[name])
-        return carry
-
-    lax.fori_loop(min(lags), chunks + max(lags), loop, 0)
+        bits, counts = carry
+        next_bits, next_counts = [], []
+        for name, word, bit, count in zip(ORDER, words, bits, counts):
+            for w in range(1, len(word)):
+                bit = jnp.where(step == w * SPAN, word[w], bit)
+            on = bit % 2
+
+            @pl.when(on == 1)
+            def _():
+                stages[name](count)
+
+            next_bits.append(bit // 2)
+            next_counts.append(count + on)
+        return tuple(next_bits), tuple(next_counts)
+
+    start = tuple(jnp.int32(word[0]) for word in words), tuple(jnp.int32(0) for _ in words)
+    lax.fori_loop(0, total, loop, start)
 
     for q in range(half_chunks):
         copy(SEND_OUT, q, out_s.at[q], out_r.at[q], far).wait_recv()
@@ -240,9 +273,8 @@
     rows, width = gradient.shape
     chunks = 2 * rows // W
     block = pltpu.VMEM((chunks, W, width), BF16)
-    wide = pltpu.VMEM((chunks, W, width), F32)
     ring = pltpu.VMEM((chunks, RING, W, width), BF16)
-    part = pltpu.VMEM((RING, W, width), F32)
+    part = pltpu.VMEM((chunks, RING, W, width), F32)
     out_block = pltpu.VMEM((chunks // 2, W, width), BF16)
     return pl.pallas_call(
         functools.partial(kernel, rows),
@@ -252,8 +284,8 @@
         scratch_shapes=[
             pltpu.VMEM((rows, width), F32),
             pltpu.VMEM((2 * precond.shape[0], width), BF16),
-            ring, part, wide, block, block, block, block, block, block, block, block,
-            ring, part, wide, block, block, block, block, block, block,
+            ring, part, block, block, block, block, block, block, block, block,
+            ring, part, block, block, block, block, block, block,
             out_block, out_block,
             pltpu.SemaphoreType.DMA((2,)),
             pltpu.SemaphoreType.DMA,

time: 118 us -> 98.7 us (0.84)
  Pallas kernels: 116 us -> 96.4 us
    pallas_call x1, Pallas kernels: 116 us -> 96.4 us  [local(): pl.pallas_call(functools.partial(kernel, rows), out_shape=jax.ShapeDtypeS...]
where the time goes in v2:
time: 98.7 us; the launch traced here: 98.6 us
  Pallas kernels  96.4 us (98%)
  local copies, waits for them, and re-layouts  2.16 us (2%)
    pallas_call x1, Pallas kernels, local(): pl.pallas_call(functools.partial(kernel, rows), out_shape=jax.ShapeDtypeS...  96.4 us
    unnamed x1, local copies, waits for them, and re-layouts  2.16 us

profile of v2, /device:TPU:0, one launch (start us, length us, event | category | flops | bytes accessed | tf_op | source)
XLA Modules:
  0.0 98.6 jit_solution(1127510043414913911)
XLA Ops:
  0.0 96.4 %shard_map.28 = f32[128,1792]{1,0:T(8,128)} custom-call(f32[128,1792]{1,0:T(8,128)} %g_hbm.1, bf16[896,1792]{1,0:T(8,128)(2,1)} %q_hbm.1), custom_call_target="tpu_custom_call" | custom-call | tf_op jit(solution)/shard_map/pallas_call | solution.py:279
  96.4 2.2 %copy.4 = f32[128,1792]{1,0:T(8,128)} copy(f32[128,1792]{1,0:T(8,128)} %shard_map.28) | data formatting | bytes 1835008

commit v3 on v2

v3 whole, which is shorter than its diff:
```python
import functools

import jax
import jax.numpy as jnp
from jax import lax
from jax.experimental import pallas as pl
from jax.experimental.pallas import tpu as pltpu
from jax.sharding import PartitionSpec as P

MESH = pl.DeviceIdType.MESH
BF16, F32 = jnp.bfloat16, jnp.float32

W = 32
TILE = 256
RING = 4
EARLY = 2
FLIP = (3,)
PARTS = 4
SPAN = 30

GATHER_X, SEND_G, SCATTER_Z, PAIR, GATHER_Z, SCATTER_X, SEND_OUT, PRE, POST, KINDS = 0, 6, 7, 13, 14, 20, 26, 27, 28, 29

ORDER = (
    "enter", "to_pair", "relay", "relay2", "hop2",
    "first", "hop1", "merge", "round_first", "second",
    "end", "spread",
)
STEPS = {
    "enter": (0, 1, 2, 3, 7, 10, 11, 12),
    "to_pair": (8, 11, 12, 17, 21, 22, 25, 27),
    "relay": (1, 2, 4, 5, 9, 12, 13, 15),
    "relay2": (12, 18, 19, 20, 26, 27, 30, 31),
    "hop2": (17, 25, 27, 28, 31, 33, 36, 37),
    "first": (3, 6, 7, 8, 11, 16, 21, 22),
    "hop1": (5, 8, 9, 13, 14, 18, 23, 24),
    "merge": (12,),
    "round_first": (10, 12, 15, 23, 25, 27, 29),
    "second": (15, 21, 24, 26, 28, 29, 33, 34),
    "end": (22, 27, 31, 32, 34, 35, 37, 38),
    "spread": (22,),
}


def pick(count, items):
    value = jnp.int32(items[0])
    for k in range(1, len(items)):
        value = jnp.where(count == k, items[k], value)
    return value


def kernel(rows, g_hbm, q_hbm, out, g_wide, factor, factor_t, gath, part, hop_s, plus_s, minus_s, hop_r, plus_r,
           minus_r, pair_s, pair_r, mid, part2, hop2_s, plus2_s, minus2_s, hop2_r, plus2_r, minus2_r,
           out_s, out_r, pre_s, pre_r, total_v, local_sem, core_send, core_recv, ss, rs):
    half_chunks = rows // W
    chunks = 2 * half_chunks
    width = factor.shape[1]
    r, c = lax.axis_index("row"), lax.axis_index("col")
    core = r % 2
    x = (r // 2) % RING
    yh = r // (2 * RING)
    z = c % RING
    yl = c // RING

    def at(yh, x, core, yl, z):
        return ((yh * RING + x) * 2 + core, yl * RING + z)

    xr, xl, xo = (x + 1) % RING, (x + 3) % RING, (x + 2) % RING
    zr, zl, zo = (z + 1) % RING, (z + 3) % RING, (z + 2) % RING
    x_plus, x_minus = at(yh, xr, core, yl, z), at(yh, xl, core, yl, z)
    z_plus, z_minus = at(yh, x, core, yl, zr), at(yh, x, core, yl, zl)
    far = at(1 - yh, x, core, yl, z)
    pair = at(yh, x, core, 1 - yl, z)
    twin = at(yh, x, 1 - core, yl, z)

    depth = q_hbm.shape[0]
    mine = pl.ds(pl.multiple_of(core * depth, depth), depth)
    theirs = pl.ds(pl.multiple_of((1 - core) * depth, depth), depth)
    lo, hi = pl.ds(0, width // 2), pl.ds(width // 2, width // 2)
    whole = pl.ds(0, W)
    kept = pl.ds(pl.multiple_of(yl * (W // 2), W // 2), W // 2)
    given = pl.ds(pl.multiple_of((1 - yl) * (W // 2), W // 2), W // 2)

    load_g = pltpu.make_async_copy(g_hbm, g_wide, local_sem.at[0])
    load_q = pltpu.make_async_copy(q_hbm, factor.at[mine], local_sem.at[1])
    load_g.start()
    load_q.start()

    barrier = pltpu.get_barrier_semaphore()
    for device in (x_plus, x_minus, z_plus, z_minus, far, pair, twin):
        pl.semaphore_signal(barrier, inc=1, device_id=device, device_id_type=MESH)
    pl.semaphore_wait(barrier, 7)

    def factor_copy(side):
        return pltpu.make_async_remote_copy(
            src_ref=q_hbm, dst_ref=factor.at[side], send_sem=core_send, recv_sem=core_recv,
            device_id=twin, device_id_type=MESH)

    factor_copy(mine).start()

    def copy(kind, i, src, dst, device):
        return pltpu.make_async_remote_copy(
            src_ref=src, dst_ref=dst, send_sem=ss.at[kind, i], recv_sem=rs.at[kind, i],
            device_id=device, device_id_type=MESH)

    def gather_send(kind, i, buf, me, plus, minus, part_rows=whole):
        for k, cols, device in ((0, lo, plus), (1, hi, minus), (2, hi, plus), (3, lo, minus)):
            piece = buf.at[i, me, part_rows, cols]
            copy(kind + k, i, piece, piece, device).start()

    def gather_relay(kind, i, buf, left, right, plus, minus, part_rows=whole):
        for k, block, cols, device in ((0, left, lo, plus), (1, right, hi, minus)):
            piece = buf.at[i, block, part_rows, cols]
            copy(kind + k, i, piece, piece, device).wait_recv()
            copy(kind + 4 + k, i, piece, piece, device).start()

    def gather_wait(kind, i, buf, left, right, across, plus, minus, part_rows=whole):
        for k, block, cols in ((2, left, hi), (3, right, lo), (4, across, lo), (5, across, hi)):
            piece = buf.at[i, block, part_rows, cols]
            copy(kind + k, i, piece, piece, plus).wait_recv()

    def scatter_send(kind, i, p, hs, ps, ms, hr, pr, mr, left, right, across, plus, minus, part_rows=whole):
        hs[i, part_rows] = p[i % PARTS, across, part_rows].astype(BF16)
        copy(kind, i, hs.at[i, part_rows, lo], hr.at[i, part_rows, lo], plus).start()
        copy(kind + 1, i, hs.at[i, part_rows, hi], hr.at[i, part_rows, hi], minus).start()
        ps[i, part_rows, hi] = p[i % PARTS, right, part_rows, hi].astype(BF16)
        copy(kind + 2, i, ps.at[i, part_rows, hi], pr.at[i, part_rows, hi], plus).start()
        ms[i, part_rows, lo] = p[i % PARTS, left, part_rows, lo].astype(BF16)
        copy(kind + 3, i, ms.at[i, part_rows, lo], mr.at[i, part_rows, lo], minus).start()

    def scatter_hop(kind, i, p, hs, ps, ms, hr, pr, mr, left, right, plus, minus, part_rows=whole):
        copy(kind, i, hs.at[i, part_rows, lo], hr.at[i, part_rows, lo], plus).wait_recv()
        ps[i, part_rows, lo] = (p[i % PARTS, right, part_rows, lo] + hr[i, part_rows, lo].astype(F32)).astype(BF16)
        copy(kind + 4, i, ps.at[i, part_rows, lo], pr.at[i, part_rows, lo], plus).start()
        copy(kind + 1, i, hs.at[i, part_rows, hi], hr.at[i, part_rows, hi], minus).wait_recv()
        ms[i, part_rows, hi] = (p[i % PARTS, left, part_rows, hi] + hr[i, part_rows, hi].astype(F32)).astype(BF16)
        copy(kind + 5, i, ms.at[i, part_rows, hi], mr.at[i, part_rows, hi], minus).start()

    def scatter_wait(kind, i, p, me, pr, mr, plus, part_rows=whole):
        for k, buf, cols in ((2, pr, hi), (3, mr, lo), (4, pr, lo), (5, mr, hi)):
            piece = buf.at[i, part_rows, cols]
            copy(kind + k, i, piece, piece, plus).wait_recv()
        return p[i % PARTS, me, part_rows] + pr[i, part_rows].astype(F32) + mr[i, part_rows].astype(F32)

    def is_far(i):
        return (i >= EARLY) & (i < EARLY + half_chunks)

    def is_flip(i):
        flag = i < 0
        for f in FLIP:
            flag = flag | (i == f)
        return flag

    def flip_slot(i):
        slot = jnp.int32(0)
        for f in FLIP[1:]:
            slot = slot + (i >= f).astype(jnp.int32)
        return slot

    def choose(flag, yes, no):
        pl.when(flag)(yes)
        pl.when(jnp.logical_not(flag))(no)

    load_g.wait()
    for q in range(half_chunks):
        i = q if q < EARLY else half_chunks + q
        gath[i, x] = g_wide[q * W:(q + 1) * W].astype(BF16)
        if i == 0:
            gather_send(GATHER_X, i, gath, x, x_plus, x_minus)
        copy(SEND_G, EARLY + q, gath.at[i, x], gath.at[EARLY + q, x], far).start()
    load_q.wait()
    factor_t[:, mine] = factor[mine, :].T

    def enter(i):
        @pl.when(is_far(i))
        def _():
            copy(SEND_G, i, gath.at[i, x], gath.at[i, x], far).wait_recv()

        @pl.when(i > 0)
        def _():
            gather_send(GATHER_X, i, gath, x, x_plus, x_minus)

    def relay(i):
        gather_relay(GATHER_X, i, gath, xl, xr, x_plus, x_minus)

    def z_send(i, part_rows):
        scatter_send(SCATTER_Z, i, part, hop_s, plus_s, minus_s, hop_r, plus_r, minus_r,
                     zl, zr, zo, z_plus, z_minus, part_rows)

    def first(i):
        gather_wait(GATHER_X, i, gath, xl, xr, xo, x_plus, x_minus)

        @pl.when(i == 0)
        def _():
            factor_copy(theirs).wait_recv()
            lhs = gath[0].reshape(RING * W, width)
            for t in range(0, width, TILE):
                value = lax.dot_general(
                    lhs, factor[t:t + TILE, :], (((1,), (1,)), ((), ())), preferred_element_type=F32)
                part[0, :, :, t:t + TILE] = value.reshape(RING, W, TILE)
            z_send(0, whole)
            factor_t[:, theirs] = factor[theirs, :].T

        @pl.when(i > 0)
        def _():
            lhs = gath[i].reshape(RING * W, width)
            for t in range(0, width, TILE):
                value = jnp.dot(lhs, factor_t[:, t:t + TILE], preferred_element_type=F32)
                part[i % PARTS, :, :, t:t + TILE] = value.reshape(RING, W, TILE)

            def exchange():
                slot = flip_slot(i)
                pre_s[slot] = part[i % PARTS, :, given].astype(BF16)
                copy(PRE, slot, pre_s.at[slot], pre_r.at[slot], pair).start()

            choose(is_flip(i), exchange, lambda: z_send(i, whole))

    def merge(count):
        i = pick(count, FLIP)
        copy(PRE, count, pre_s.at[count], pre_r.at[count], pair).wait_recv()
        part[i % PARTS, :, kept] += pre_r[count].astype(F32)
        z_send(i, kept)

    def hop1(i):
        def run(part_rows):
            scatter_hop(SCATTER_Z, i, part, hop_s, plus_s, minus_s, hop_r, plus_r, minus_r,
                        zl, zr, z_plus, z_minus, part_rows)

        choose(is_flip(i), lambda: run(kept), lambda: run(whole))

    def to_pair(i):
        def flipped():
            value = scatter_wait(SCATTER_Z, i, part, z, plus_r, minus_r, z_plus, kept)
            mid[i, z, kept] = value.astype(BF16)
            gather_send(GATHER_Z, i, mid, z, z_plus, z_minus, kept)

        def plain():
            value = scatter_wait(SCATTER_Z, i, part, z, plus_r, minus_r, z_plus)
            part[i % PARTS, z] = value
            pair_s[i] = value.astype(BF16)
            copy(PAIR, i, pair_s.at[i], pair_r.at[i], pair).start()

        choose(is_flip(i), flipped, plain)

    def round_first(count):
        i = pick(count, [k for k in range(chunks) if k not in FLIP])
        copy(PAIR, i, pair_s.at[i], pair_r.at[i], pair).wait_recv()
        mid[i, z] = (part[i % PARTS, z] + pair_r[i].astype(F32)).astype(BF16)
        gather_send(GATHER_Z, i, mid, z, z_plus, z_minus)

    def relay2(i):
        def run(part_rows):
            gather_relay(GATHER_Z, i, mid, zl, zr, z_plus, z_minus, part_rows)

        choose(is_flip(i), lambda: run(kept), lambda: run(whole))

    def spread(count):
        i = pick(count, FLIP)
        gather_wait(GATHER_Z, i, mid, zl, zr, zo, z_plus, z_minus, kept)
        copy(POST, count, mid.at[i, :, kept], mid.at[i, :, kept], pair).start()

    def second(i):
        def flipped():
            piece = mid.at[i, :, given]
            copy(POST, flip_slot(i), piece, piece, pair).wait_recv()

        choose(is_flip(i), flipped, lambda: gather_wait(GATHER_Z, i, mid, zl, zr, zo, z_plus, z_minus))
        lhs = mid[i].reshape(RING * W, width)
        for t in range(0, width, TILE):
            value = jnp.dot(lhs, factor[:, t:t + TILE], preferred_element_type=F32)
            part2[i % PARTS, :, :, t:t + TILE] = value.reshape(RING, W, TILE)
        scatter_send(SCATTER_X, i, part2, hop2_s, plus2_s, minus2_s, hop2_r, plus2_r, minus2_r,
                     xl, xr, xo, x_plus, x_minus)

    def hop2(i):
        scatter_hop(SCATTER_X, i, part2, hop2_s, plus2_s, minus2_s, hop2_r, plus2_r, minus2_r,
                    xl, xr, x_plus, x_minus)

    def end(i):
        value = scatter_wait(SCATTER_X, i, part2, x, plus2_r, minus2_r, x_plus)

        def away():
            q = i - EARLY
            out_s[q] = value.astype(BF16)
            copy(SEND_OUT, q, out_s.at[q], out_r.at[q], far).start()

        def here():
            q = jnp.where(i < EARLY, i, i - half_chunks)
            total_v[pl.ds(pl.multiple_of(q * W, W), W), :] = value

        choose(is_far(i), away, here)

    stages = {
        "enter": enter, "relay": relay, "first": first, "merge": merge, "hop1": hop1, "to_pair": to_pair,
        "round_first": round_first, "relay2": relay2, "spread": spread, "second": second, "hop2": hop2, "end": end,
    }
    total = 1 + max(max(at_steps) for at_steps in STEPS.values())
    words = [
        [sum(1 << (t - w) for t in STEPS[name] if w <= t < w + SPAN) for w in range(0, total, SPAN)]
        for name in ORDER
    ]

    def loop(step, carry):
        bits, counts = carry
        next_bits, next_counts = [], []
        for name, word, bit, count in zip(ORDER, words, bits, counts):
            for w in range(1, len(word)):
                bit = jnp.where(step == w * SPAN, word[w], bit)
            on = bit % 2

            @pl.when(on == 1)
            def _():
                stages[name](count)

            next_bits.append(bit // 2)
            next_counts.append(count + on)
        return tuple(next_bits), tuple(next_counts)

    start = tuple(jnp.int32(word[0]) for word in words), tuple(jnp.int32(0) for _ in words)
    lax.fori_loop(0, total, loop, start)

    def store(q):
        band = pl.ds(q * W, W)
        return pltpu.make_async_copy(total_v.at[band], out.at[band], local_sem.at[2 + q])

    for q in range(half_chunks):
        copy(SEND_OUT, q, out_s.at[q], out_r.at[q], far).wait_recv()
        total_v[q * W:(q + 1) * W] += out_r[q].astype(F32)
        store(q).start()

    factor_copy(mine).wait_send()

    def sent(kind, i, piece):
        copy(kind, i, piece, piece, pair).wait_send()

    def drain(i, carry):
        for kind in (GATHER_X, SCATTER_X):
            for k in range(6):
                sent(kind + k, i, hop_s.at[i, whole, lo])

        def drain_z(part_rows):
            for kind in (GATHER_Z, SCATTER_Z):
                for k in range(6):
                    sent(kind + k, i, hop_s.at[i, part_rows, lo])

        def flipped():
            drain_z(kept)
            slot = flip_slot(i)
            sent(PRE, slot, pre_s.at[slot])
            sent(POST, slot, pre_s.at[slot])

        def plain():
            drain_z(whole)
            sent(PAIR, i, pair_s.at[i])

        choose(is_flip(i), flipped, plain)

        @pl.when(i < half_chunks)
        def _():
            sent(SEND_G, EARLY + i, pair_s.at[i])
            sent(SEND_OUT, i, out_s.at[i])

        return carry

    lax.fori_loop(0, chunks, drain, 0)
    for q in range(half_chunks):
        store(q).wait()


def local(gradient, precond):
    rows, width = gradient.shape
    chunks = 2 * rows // W
    flips = max(1, len(FLIP))
    block = pltpu.VMEM((chunks, W, width), BF16)
    ring = pltpu.VMEM((chunks, RING, W, width), BF16)
    part = pltpu.VMEM((PARTS, RING, W, width), F32)
    out_block = pltpu.VMEM((chunks // 2, W, width), BF16)
    half_ring = pltpu.VMEM((flips, RING, W // 2, width), BF16)
    square = pltpu.VMEM((2 * precond.shape[0], width), BF16)
    return pl.pallas_call(
        functools.partial(kernel, rows),
        out_shape=jax.ShapeDtypeStruct((rows, width), F32),
        in_specs=[pl.BlockSpec(memory_space=pl.ANY)] * 2,
        out_specs=pl.BlockSpec(memory_space=pl.ANY),
        scratch_shapes=[
            pltpu.VMEM((rows, width), F32),
            square, square,
            ring, part, block, block, block, block, block, block, block, block,
            ring, part, block, block, block, block, block, block,
            out_block, out_block, half_ring, half_ring,
            pltpu.VMEM((rows, width), F32),
            pltpu.SemaphoreType.DMA((2 + chunks // 2,)),
            pltpu.SemaphoreType.DMA,
            pltpu.SemaphoreType.DMA,
            pltpu.SemaphoreType.DMA((KINDS, chunks)),
            pltpu.SemaphoreType.DMA((KINDS, chunks)),
        ],
        compiler_params=pltpu.CompilerParams(
            collective_id=0, has_side_effects=True, vmem_limit_bytes=50 * 1024 * 1024
        ),
    )(gradient, precond)


def solution(mesh):
    placed = (P("row", "col"), P("row", "col"))
    return jax.shard_map(
        local, mesh=mesh, in_specs=placed, out_specs=P("row", "col"), check_vma=False
    )
```

time: 98.7 us -> 94.8 us (0.960)
  Pallas kernels: 96.4 us -> 92.5 us
    pallas_call x1, Pallas kernels: 96.4 us -> 92.5 us  [local(): pl.pallas_call(functools.partial(kernel, rows), out_shape=jax.ShapeDtypeS...]
    unnamed x1 -> x3, local copies, waits for them, and re-layouts: 2.16 us -> 2.1 us
where the time goes in v3:
time: 94.8 us; the launch traced here: 94.6 us
  Pallas kernels  92.5 us (98%)
  local copies, waits for them, and re-layouts  2.1 us (2%)
    pallas_call x1, Pallas kernels, local(): pl.pallas_call(functools.partial(kernel, rows), out_shape=jax.ShapeDtypeS...  92.5 us
    unnamed x3, local copies, waits for them, and re-layouts  2.1 us

profile of v3, /device:TPU:0, one launch (start us, length us, event | category | flops | bytes accessed | tf_op | source)
XLA Modules:
  0.0 94.6 jit_solution(11352536336798148016)
XLA Ops:
  0.0 0.0 copy-start
  0.0 1.2 %copy-done = f32[128,1792]{1,0:T(8,128)S(1)} copy-done((f32[128,1792]{1,0:T(8,128)S(1)}, f32[128,1792]{1,0:T(8,128)}, u32[]{:S(2)}) %copy-start) | copy-done | bytes 917528
  1.2 92.5 %shard_map.28 = f32[128,1792]{1,0:T(8,128)S(1)} custom-call(f32[128,1792]{1,0:T(8,128)S(1)} %copy-done, bf16[896,1792]{1,0:T(8,128)(2,1)} %q_hbm.1), custom_call_target="tpu_custom_call" | custom-call | tf_op jit(solution)/shard_map/pallas_call | solution.py:379
  93.7 0.9 copy.4
Async XLA Ops:
  0.0 1.2 %copy-start = (f32[128,1792]{1,0:T(8,128)S(1)}, f32[128,1792]{1,0:T(8,128)}, u32[]{:S(2)}) copy-start(f32[128,1792]{1,0:T(8,128)} %g_hbm.1) | copy-start | bytes 2752516

commit v4 on v3

--- a/solution.py
+++ b/solution.py
@@ -191,12 +191,19 @@
 
         @pl.when(i == 0)
         def _():
+            lhs = gath[0].reshape(RING * W, width)
+            for t in range(0, depth, 256):
+                tile = min(256, depth - t)
+                cols = pl.ds(pl.multiple_of(core * depth + t, 128), tile)
+                value = jnp.dot(lhs, factor_t[:, cols], preferred_element_type=F32)
+                part[0, :, :, cols] = value.reshape(RING, W, tile)
             factor_copy(theirs).wait_recv()
-            lhs = gath[0].reshape(RING * W, width)
-            for t in range(0, width, TILE):
+            for t in range(0, depth, 256):
+                tile = min(256, depth - t)
+                cols = pl.ds(pl.multiple_of((1 - core) * depth + t, 128), tile)
                 value = lax.dot_general(
-                    lhs, factor[t:t + TILE, :], (((1,), (1,)), ((), ())), preferred_element_type=F32)
-                part[0, :, :, t:t + TILE] = value.reshape(RING, W, TILE)
+                    lhs, factor[cols, :], (((1,), (1,)), ((), ())), preferred_element_type=F32)
+                part[0, :, :, cols] = value.reshape(RING, W, tile)
             z_send(0, whole)
             factor_t[:, theirs] = factor[theirs, :].T
 
@@ -395,7 +402,7 @@
             pltpu.SemaphoreType.DMA((KINDS, chunks)),
         ],
         compiler_params=pltpu.CompilerParams(
-            collective_id=0, has_side_effects=True, vmem_limit_bytes=50 * 1024 * 1024
+            collective_id=0, has_side_effects=True, vmem_limit_bytes=53 * 1024 * 1024
         ),
     )(gradient, precond)
 

time: 94.8 us -> 92.8 us (0.979)
  local copies, waits for them, and re-layouts: 2.1 us -> 0.93 us
    unnamed x3 -> x1, local copies, waits for them, and re-layouts: 2.1 us -> 0.93 us
where the time goes in v4:
time: 92.8 us; the launch traced here: 92.7 us
  Pallas kernels  91.8 us (99%)
  local copies, waits for them, and re-layouts  0.93 us (1%)
    pallas_call x1, Pallas kernels, local(): pl.pallas_call(functools.partial(kernel, rows), out_shape=jax.ShapeDtypeS...  91.8 us

profile of v4, /device:TPU:0, one launch (start us, length us, event | category | flops | bytes accessed | tf_op | source)
XLA Modules:
  0.0 92.7 jit_solution(3272537189242608409)
XLA Ops:
  0.0 91.8 %shard_map.28 = f32[128,1792]{1,0:T(8,128)S(1)} custom-call(f32[128,1792]{1,0:T(8,128)} %g_hbm.1, bf16[896,1792]{1,0:T(8,128)(2,1)} %q_hbm.1), custom_call_target="tpu_custom_call" | custom-call | tf_op jit(solution)/shard_map/pallas_call | solution.py:386
  91.8 0.9 copy.4

commit v5 on v4

--- a/solution.py
+++ b/solution.py
@@ -160,6 +160,35 @@
         pl.when(flag)(yes)
         pl.when(jnp.logical_not(flag))(no)
 
+    def sent(kind, i, piece):
+        copy(kind, i, piece, piece, pair).wait_send()
+
+    def drain(i):
+        for kind in (GATHER_X, SCATTER_X):
+            for k in range(6):
+                sent(kind + k, i, hop_s.at[i, whole, lo])
+
+        def drain_z(part_rows):
+            for kind in (GATHER_Z, SCATTER_Z):
+                for k in range(6):
+                    sent(kind + k, i, hop_s.at[i, part_rows, lo])
+
+        def flipped():
+            drain_z(kept)
+            slot = flip_slot(i)
+            sent(PRE, slot, pre_s.at[slot])
+            sent(POST, slot, pre_s.at[slot])
+
+        def plain():
+            drain_z(whole)
+            sent(PAIR, i, pair_s.at[i])
+
+        choose(is_flip(i), flipped, plain)
+
+        @pl.when(is_far(i))
+        def _():
+            sent(SEND_G, i, pair_s.at[i])
+
     load_g.wait()
     for q in range(half_chunks):
         i = q if q < EARLY else half_chunks + q
@@ -296,6 +325,10 @@
 
         choose(is_far(i), away, here)
 
+        @pl.when(i > 0)
+        def _():
+            drain(i - 1)
+
     stages = {
         "enter": enter, "relay": relay, "first": first, "merge": merge, "hop1": hop1, "to_pair": to_pair,
         "round_first": round_first, "relay2": relay2, "spread": spread, "second": second, "hop2": hop2, "end": end,
@@ -336,39 +369,9 @@
 
     factor_copy(mine).wait_send()
 
-    def sent(kind, i, piece):
-        copy(kind, i, piece, piece, pair).wait_send()
-
-    def drain(i, carry):
-        for kind in (GATHER_X, SCATTER_X):
-            for k in range(6):
-                sent(kind + k, i, hop_s.at[i, whole, lo])
-
-        def drain_z(part_rows):
-            for kind in (GATHER_Z, SCATTER_Z):
-                for k in range(6):
-                    sent(kind + k, i, hop_s.at[i, part_rows, lo])
-
-        def flipped():
-            drain_z(kept)
-            slot = flip_slot(i)
-            sent(PRE, slot, pre_s.at[slot])
-            sent(POST, slot, pre_s.at[slot])
-
-        def plain():
-            drain_z(whole)
-            sent(PAIR, i, pair_s.at[i])
-
-        choose(is_flip(i), flipped, plain)
-
-        @pl.when(i < half_chunks)
-        def _():
-            sent(SEND_G, EARLY + i, pair_s.at[i])
-            sent(SEND_OUT, i, out_s.at[i])
-
-        return carry
-
-    lax.fori_loop(0, chunks, drain, 0)
+    drain(jnp.int32(chunks - 1))
+    for q in range(half_chunks):
+        sent(SEND_OUT, q, out_s.at[q])
     for q in range(half_chunks):
         store(q).wait()
 

time: 92.8 us -> 92.5 us (level)
  no operation moved by 1% of the time
where the time goes in v5:
time: 92.5 us; the launch traced here: 92.4 us
  Pallas kernels  91.5 us (99%)
  local copies, waits for them, and re-layouts  0.93 us (1%)
    pallas_call x1, Pallas kernels, local(): pl.pallas_call(functools.partial(kernel, rows), out_shape=jax.ShapeDtypeS...  91.5 us

profile of v5, /device:TPU:0, one launch (start us, length us, event | category | flops | bytes accessed | tf_op | source)
XLA Modules:
  0.0 92.4 jit_solution(6096948151514749988)
XLA Ops:
  0.0 91.5 %shard_map.28 = f32[128,1792]{1,0:T(8,128)S(1)} custom-call(f32[128,1792]{1,0:T(8,128)} %g_hbm.1, bf16[896,1792]{1,0:T(8,128)(2,1)} %q_hbm.1), custom_call_target="tpu_custom_call" | custom-call | tf_op jit(solution)/shard_map/pallas_call | solution.py:389
  91.5 0.9 %copy.4 = f32[128,1792]{1,0:T(8,128)} copy(f32[128,1792]{1,0:T(8,128)S(1)} %shard_map.28) | data formatting | bytes 1835008
